TPU v7x, 256 devices: a whole 4x4x8 slice. The times are simulated.
256 devices in a mesh: row: 8 (over z), col: 32 (over y, x, core).
Axes of the slice: x: 4, y: 4, z: 8, core: 2. Of those that a mesh axis runs over, the one named last changes fastest.
Arguments:
- matrix: float32 [16384, 16384], P('row', 'col'), may hold values from -48 to 48, as said below
- pivots: int32 [2, 64], replicated, may hold values from 128 to 16383, as said below
Outputs:
- factored: float32 [16384, 16384], P('row', 'col')
Inputs may be any that keep to these rules, and one draw needn't show every extreme that they name: `pivots`: the 128 entries are distinct global row numbers. `matrix`: the entry of row pivots[c, k] in global column c * 64 + k dominates the other entries of its global column, so that multipliers stay well below one.
All inputs are finite; a program needn't handle non-finite values.
Results may differ from a plain program's by a relative error of at most 0.0002.
Values sent between devices are 32-bit elements; how exact they have to be, the bound alone decides.
A program may use at most 64 MiB of HBM per device.

v0:
```python
import jax
import jax.numpy as jnp
from jax import lax
from jax.sharding import PartitionSpec as P

NB = 64
HIGHEST_PRECISION = lax.Precision.HIGHEST


def from_root(value, axis, source):
    kept = jnp.where(lax.axis_index(axis) == source, value, 0).astype(value.dtype)
    return lax.psum(kept, axis)


def eliminate(panel_t):
    panel_width, row_count = panel_t.shape
    row_ids = jnp.arange(row_count, dtype=jnp.int32)
    col_ids = jnp.arange(panel_width, dtype=jnp.int32)

    def eliminate_step(column, current):
        pivot_line = lax.dynamic_index_in_dim(current, column, 1, keepdims=False)
        pivot_value = lax.dynamic_index_in_dim(pivot_line, column, 0, keepdims=False)
        weight = 1.0 / pivot_value
        column_line = lax.dynamic_index_in_dim(current, column, 0, keepdims=False)
        below_rows = row_ids > column
        multiplier = jnp.where(below_rows, column_line * weight, 0.0)
        later_part = jnp.where(col_ids > column, pivot_line, 0.0)
        current = current - later_part[:, None] * multiplier[None, :]
        return jnp.where(
            (col_ids == column)[:, None] & below_rows[None, :], multiplier[None, :], current
        )

    return lax.fori_loop(0, panel_width, eliminate_step, panel_t)


def solve_rows(top_t, right_side):
    unit_part = jnp.tril(top_t.T, -1) + jnp.eye(top_t.shape[0], dtype=top_t.dtype)
    return lax.linalg.triangular_solve(
        unit_part, right_side, left_side=True, lower=True, unit_diagonal=True
    )


def fetch_rows(local_matrix, global_rows, my_row, grid_rows):
    block_ids = global_rows // NB
    owned = block_ids % grid_rows == my_row
    local_index = block_ids // grid_rows * NB + global_rows % NB
    row_values = jnp.where(owned[:, None], local_matrix[jnp.where(owned, local_index, 0)], 0.0)
    return (row_values, jnp.where(owned, local_index, local_matrix.shape[0]))


def place_rows(local_matrix, local_index, row_values):
    return local_matrix.at[local_index].set(row_values, mode="drop")


def apply_panel(
    local_matrix,
    panel,
    lower_t,
    top_t,
    upper_rows,
    row_blocks,
    col_blocks,
    my_row,
    my_col,
    grid_rows,
    grid_cols,
):
    below_rows = row_blocks > panel
    right_cols = col_blocks > panel
    product = lax.dot_general(
        lower_t,
        upper_rows,
        (((0,), (0,)), ((), ())),
        precision=HIGHEST_PRECISION,
        preferred_element_type=jnp.float32,
    )
    result = jnp.where(
        below_rows[:, None] & right_cols[None, :], local_matrix - product, local_matrix
    )
    col_start = panel // grid_cols * NB
    row_start = panel // grid_rows * NB
    owns_col = my_col == panel % grid_cols
    owns_row = my_row == panel % grid_rows
    col_part = jnp.where(
        below_rows[:, None] & owns_col, lower_t.T, result[:, col_start : col_start + NB]
    )
    result = result.at[:, col_start : col_start + NB].set(col_part)
    row_part = jnp.where(
        right_cols[None, :] & owns_row, upper_rows, result[row_start : row_start + NB]
    )
    result = result.at[row_start : row_start + NB].set(row_part)
    corner = jnp.where(
        owns_row & owns_col, top_t.T, result[row_start : row_start + NB, col_start : col_start + NB]
    )
    return result.at[row_start : row_start + NB, col_start : col_start + NB].set(corner)


def shards(matrix, pivots):
    rows_dev, cols_dev = matrix.shape
    grid_rows = lax.axis_size("row")
    grid_cols = lax.axis_size("col")
    my_row = lax.axis_index("row")
    my_col = lax.axis_index("col")
    row_blocks = jnp.arange(rows_dev, dtype=jnp.int32) // NB * grid_rows + my_row
    col_blocks = jnp.arange(cols_dev, dtype=jnp.int32) // NB * grid_cols + my_col
    local_matrix = matrix
    for panel in range(2):
        top_global = panel * NB + jnp.arange(NB, dtype=jnp.int32)
        pivot_values, pivot_index = fetch_rows(local_matrix, pivots[panel], my_row, grid_rows)
        top_values, top_index = fetch_rows(local_matrix, top_global, my_row, grid_rows)
        new_top, new_pivot = lax.psum((pivot_values, top_values), "row")
        local_matrix = place_rows(
            place_rows(local_matrix, top_index, new_top), pivot_index, new_pivot
        )
        col_start = panel // grid_cols * NB
        panel_t = jnp.concatenate(
            [
                new_top[:, col_start : col_start + NB].T,
                local_matrix[:, col_start : col_start + NB].T,
            ],
            axis=1,
        )
        factored_panel = eliminate(panel_t)
        lower_t, top_t = (
            from_root(factored_panel[:, NB:], "col", panel % grid_cols),
            from_root(factored_panel[:, :NB], "col", panel % grid_cols),
        )
        upper_rows = solve_rows(top_t, new_top)
        local_matrix = apply_panel(
            local_matrix,
            panel,
            lower_t,
            top_t,
            upper_rows,
            row_blocks,
            col_blocks,
            my_row,
            my_col,
            grid_rows,
            grid_cols,
        )
    return local_matrix


def solution(mesh):
    placed = (P("row", "col"), P())
    return jax.shard_map(
        shards, mesh=mesh, in_specs=placed, out_specs=P("row", "col"), check_vma=False
    )
```

profile of v0, /device:TPU:1, one launch (start us, length us, event | category | flops | bytes accessed | tf_op | source)
XLA Modules:
  0.0 983.9 jit_solution(361981040310378852)
XLA Ops:
  6.5 4.7 copy.48
  11.3 2.9 gather_fusion.1
  14.2 2.9 gather_fusion
  17.1 0.7 broadcast_select_fusion.2
  17.8 0.7 broadcast_select_fusion.3
  18.8 0.7 compare_reduce_fusion
  19.5 70.9 %all-reduce.13.cloned.1.call-done = (f32[64,512]{1,0:T(8,128)}, f32[64,512]{1,0:T(8,128)}) async-done(((f32[64,512]{1,0:T(8,128)}, f32[64,512]{1,0:T(8,128)}), (f32[64,512]{1,0:T(8,128)}, f32[64,512]{1,0:T(8,128)})) %all-reduce.13.cloned.1.call-update) | async-done | bytes 262160 | tf_op jit(solution)/shard_map/psum | solution.py:111
  90.5 0.8 slice_bitcast_fusion.3
  91.2 5.3 scatter_fusion
  96.6 5.3 scatter_fusion.1
  101.9 1.3 slice_bitcast_fusion.1
  103.6 133.3 %while.42 = (s32[]{:T(128)}, f32[64,2112]{1,0:T(8,128)S(1)}, s32[]{:T(128)}, f32[1,1]{1,0:T(1,128)}, s32[]{:T(128)}, /*index=5*/s32[]{:T(128)}, s32[]{:T(128)}) while((s32[]{:T(128)}, f32[64,2112]{1,0:T(8,128)S(1)}, s32[]{:T(128)}, f32[1,1]{1,0:T(1,128)}, s32[]{:T(128)}, /*index=5*/s32[]{:T(128)}, s32[]{:T(128)}) %tuple.126), condition=%wide.region_5.6_spmd.clone.clone, body=%wide.region_4.5_spmd.clone.clone.sunk | while | flops 547205 | bytes 2196437 | solution.py:33
  103.6 0.7 dynamic_slice.81
  105.7 0.7 dynamic_slice.81
  107.8 0.7 dynamic_slice.81
  109.9 0.7 dynamic_slice.81
  111.9 0.7 dynamic_slice.81
  114.0 0.7 dynamic_slice.81
  116.1 0.7 dynamic_slice.81
  118.2 0.7 dynamic_slice.81
  120.3 0.7 dynamic_slice.81
  122.4 0.7 dynamic_slice.81
  124.4 0.7 dynamic_slice.81
  126.5 0.7 dynamic_slice.81
  128.6 0.7 dynamic_slice.81
  130.7 0.7 dynamic_slice.81
  132.8 0.7 dynamic_slice.81
  134.9 0.7 dynamic_slice.81
  136.9 0.7 dynamic_slice.81
  139.0 0.7 dynamic_slice.81
  141.1 0.7 dynamic_slice.81
  143.2 0.7 dynamic_slice.81
  145.3 0.7 dynamic_slice.81
  147.4 0.7 dynamic_slice.81
  237.3 1.1 slice_select_fusion.1
  238.4 123.9 %psum.59 = f32[64,64]{1,0:T(8,128)S(1)} all-reduce(f32[64,64]{1,0:T(8,128)S(1)} %fusion.17), channel_id=1, replica_groups=mesh['row'=8,'col'=32] {'col'}, use_global_device_ids=true, to_apply=%region_7.8 | all-reduce | flops 4096 | bytes 32768 | tf_op jit(solution)/shard_map/psum | solution.py:12
  362.5 4.9 custom-call.4
  367.7 108.8 %all-reduce.7.cloned.1.call-done = f32[64,2048]{0,1:T(8,128)} async-done(((f32[64,2048]{0,1:T(8,128)}), f32[64,2048]{0,1:T(8,128)}) %all-reduce.7.cloned.1.call-update) | async-done | bytes 524304 | tf_op jit(solution)/shard_map/psum | solution.py:12
  476.5 6.4 subtract_select_fusion.3
  483.0 2.0 copy-done
  485.0 1.0 select_select_fusion.1
  486.0 5.8 scatter.60
  491.8 1.6 constant_dynamic-update-slice_fusion.1
  493.4 2.8 scatter.62
  496.2 2.9 gather_fusion.3
  499.1 2.9 gather_fusion.2
  502.0 0.7 broadcast_select_fusion
  502.8 0.7 broadcast_select_fusion.1
  503.6 67.8 %all-reduce.11.cloned.1.call-done = (f32[64,512]{1,0:T(8,128)}, f32[64,512]{1,0:T(8,128)}) async-done(((f32[64,512]{1,0:T(8,128)}, f32[64,512]{1,0:T(8,128)}), (f32[64,512]{1,0:T(8,128)}, f32[64,512]{1,0:T(8,128)})) %all-reduce.11.cloned.1.call-update) | async-done | bytes 262160 | tf_op jit(solution)/shard_map/psum | solution.py:111
  571.5 0.8 slice_bitcast_fusion.2
  572.2 5.3 scatter_fusion.2
  577.5 5.3 scatter_fusion.3
  582.9 1.3 slice_bitcast_fusion
  584.6 133.3 %while.43 = (s32[]{:T(128)}, f32[64,2112]{1,0:T(8,128)S(1)}, s32[]{:T(128)}, f32[1,1]{1,0:T(1,128)}, s32[]{:T(128)}, /*index=5*/s32[]{:T(128)}, s32[]{:T(128)}) while((s32[]{:T(128)}, f32[64,2112]{1,0:T(8,128)S(1)}, s32[]{:T(128)}, f32[1,1]{1,0:T(1,128)}, s32[]{:T(128)}, /*index=5*/s32[]{:T(128)}, s32[]{:T(128)}) %tuple.129), condition=%wide.region_14.16_spmd.clone.clone, body=%wide.region_13.15_spmd.clone.clone.sunk | while | flops 547205 | bytes 2196437 | solution.py:33
  718.3 1.1 slice_select_fusion
  719.4 124.1 %psum.63 = f32[64,64]{1,0:T(8,128)S(1)} all-reduce(f32[64,64]{1,0:T(8,128)S(1)} %fusion.16), channel_id=1, replica_groups=mesh['row'=8,'col'=32] {'col'}, use_global_device_ids=true, to_apply=%region_16.18 | all-reduce | flops 4096 | bytes 32768 | tf_op jit(solution)/shard_map/psum | solution.py:12
  843.6 4.9 custom-call.5
  848.9 108.8 %all-reduce.9.cloned.1.call-done = f32[64,2048]{0,1:T(8,128)} async-done(((f32[64,2048]{0,1:T(8,128)}), f32[64,2048]{0,1:T(8,128)}) %all-reduce.9.cloned.1.call-update) | async-done | bytes 524304 | tf_op jit(solution)/shard_map/psum | solution.py:12
  957.7 6.4 subtract_select_fusion.2
  964.1 2.0 copy-done.1
  966.2 1.0 select_select_fusion
  967.2 5.8 scatter.65
  973.0 1.6 constant_dynamic-update-slice_fusion
  974.6 2.8 scatter.67
  (927 shorter events, 153.7 us)
Async XLA Ops:
  6.5 4.7 copy-start.6
  6.5 83.9 %all-reduce.13.cloned.1.call-start = ((), (), s32[]{:S(2)}) async-start(), calls=%async_computation.3 | async-start | bytes 524288 | tf_op jit(solution)/shard_map/psum | solution.py:111
  18.6 457.9 %all-reduce.7.cloned.1.call-start = ((), (), s32[]{:S(2)}) async-start(), calls=%async_computation | async-start | bytes 2097152 | tf_op jit(solution)/shard_map/psum | solution.py:12
  236.9 130.5 %copy-start.4 = (f32[64,512]{1,0:T(8,128)S(1)}, f32[64,512]{1,0:T(8,128)}, u32[]{:S(2)}) copy-start(f32[64,512]{1,0:T(8,128)} %get-tuple-element.386) | copy-start | bytes 393220
  362.4 209.1 %all-reduce.11.cloned.1.call-start = ((), (), s32[]{:S(2)}) async-start(), calls=%async_computation.2 | async-start | bytes 524288 | tf_op jit(solution)/shard_map/psum | solution.py:111
  476.5 8.5 copy-start.2
  483.0 2.0 copy-start
  503.5 454.2 %all-reduce.9.cloned.1.call-start = ((), (), s32[]{:S(2)}) async-start(), calls=%async_computation.1 | async-start | bytes 2097152 | tf_op jit(solution)/shard_map/psum | solution.py:12
  717.9 130.6 %copy-start.5 = (f32[64,512]{1,0:T(8,128)S(1)}, f32[64,512]{1,0:T(8,128)}, u32[]{:S(2)}) copy-start(f32[64,512]{1,0:T(8,128)} %get-tuple-element.384) | copy-start | bytes 393220
  957.7 8.4 copy-start.3
  964.1 2.0 copy-start.1
Sparse Core Ops, SparseCore 0:
  18.7 71.6 all-reduce.12
  362.5 113.9 all-reduce.6
  503.6 67.7 all-reduce.10
  843.7 113.9 all-reduce.8
where the time goes:
time: 987 us; the launch traced here: 984 us
  waiting for transfers between devices  356 us (36%)
  blocking collectives  248 us (25%)
  local copies, waits for them, and re-layouts  195 us (20%)
  loops' own time  101 us (10%)
  other arithmetic  56.1 us (6%)
  matrix products  13.5 us (1%)
  between operations  13.4 us (1%)
    psum x2, blocking collectives, from_root(): return lax.psum(kept, axis)  248 us
    psum x2, waiting for transfers between devices, from_root(): return lax.psum(kept, axis)  218 us
    psum x2, waiting for transfers between devices, shards(): new_top, new_pivot = lax.psum((pivot_values, top_values), 'row')  139 us
    another operation x2, loops' own time, eliminate(): return lax.fori_loop(0, panel_width, eliminate_step, panel_t)  101 us
    dynamic_slice x128, local copies, waits for them, and re-layouts, eliminate_step(): lax.dynamic_index_in_dim(pivot_line, column, 0, keepdims=False)  85.8 us
    while x128, local copies, waits for them, and re-layouts  45.2 us
    select_n x128, other arithmetic, eliminate_step(): jnp.where((col_ids == column)[:, None] & below_rows[None, :], multiplier[...  25.8 us
    scatter x4, local copies, waits for them, and re-layouts, place_rows(): return local_matrix.at[local_index].set(row_values, mode='drop')  21.3 us
  transfers between devices with their start and end apart: 4, of which 4 were waited for; matrix products, arithmetic and copies ran while one was open for 1% of the time, Pallas kernels for 0%

commit v1 on v0

--- a/solution.py
+++ b/solution.py
@@ -9,7 +9,7 @@
 
 def from_root(value, axis, source):
     kept = jnp.where(lax.axis_index(axis) == source, value, 0).astype(value.dtype)
-    return lax.psum(kept, axis)
+    return jnp.sum(lax.all_gather(kept, axis), axis=0)
 
 
 def eliminate(panel_t):

time: 987 us -> 687 us (0.70)
  blocking collectives: 248 us -> 64.1 us
  waiting for transfers between devices: 356 us -> 228 us
  other arithmetic: 56.1 us -> 69.7 us
    psum x2 -> x0, blocking collectives: 248 us -> none  [from_root(): return lax.psum(kept, axis)]
    psum x2 -> x0, waiting for transfers between devices: 218 us -> none  [from_root(): return lax.psum(kept, axis)]
    all_gather x0 -> x2, waiting for transfers between devices: none -> 88.9 us  [from_root(): return jnp.sum(lax.all_gather(kept, axis), axis=0)]
    all_gather x0 -> x2, blocking collectives: none -> 64.1 us  [from_root(): return jnp.sum(lax.all_gather(kept, axis), axis=0)]
    reduce_sum x0 -> x4, other arithmetic: none -> 14 us  [from_root(): return jnp.sum(lax.all_gather(kept, axis), axis=0)]
    while x130 -> x128, local copies, waits for them, and re-layouts: 45.9 us -> 45.2 us
  transfers between devices with their start and end apart: 4 -> 4, of which waited for: 4 -> 4; matrix products, arithmetic and copies ran while one was open for 1% -> 2% of each run, Pallas kernels for 0% -> 0%
where the time goes in v1:
time: 687 us; the launch traced here: 684 us
  waiting for transfers between devices  228 us (33%)
  local copies, waits for them, and re-layouts  195 us (28%)
  loops' own time  101 us (15%)
  other arithmetic  69.7 us (10%)
  blocking collectives  64.1 us (9%)
  between operations  13.5 us (2%)
  matrix products  12 us (2%)
    psum x2, waiting for transfers between devices, shards(): new_top, new_pivot = lax.psum((pivot_values, top_values), 'row')  139 us
    another operation x2, loops' own time, eliminate(): return lax.fori_loop(0, panel_width, eliminate_step, panel_t)  101 us
    all_gather x2, waiting for transfers between devices, from_root(): return jnp.sum(lax.all_gather(kept, axis), axis=0)  88.9 us
    dynamic_slice x128, local copies, waits for them, and re-layouts, eliminate_step(): lax.dynamic_index_in_dim(pivot_line, column, 0, keepdims=False)  85.8 us
    all_gather x2, blocking collectives, from_root(): return jnp.sum(lax.all_gather(kept, axis), axis=0)  64.1 us
    while x128, local copies, waits for them, and re-layouts  45.2 us
    select_n x128, other arithmetic, eliminate_step(): jnp.where((col_ids == column)[:, None] & below_rows[None, :], multiplier[...  25.8 us
    scatter x4, local copies, waits for them, and re-layouts, place_rows(): return local_matrix.at[local_index].set(row_values, mode='drop')  21.3 us
  transfers between devices with their start and end apart: 4, of which 4 were waited for; matrix products, arithmetic and copies ran while one was open for 2% of the time, Pallas kernels for 0%

profile of v1, /device:TPU:1, one launch (start us, length us, event | category | flops | bytes accessed | tf_op | source)
XLA Modules:
  0.0 683.8 jit_solution(73516974612721246)
XLA Ops:
  6.5 4.7 copy.48
  11.3 2.9 gather_fusion.1
  14.2 2.9 gather_fusion
  17.1 0.7 broadcast_select_fusion.2
  17.8 0.7 broadcast_select_fusion.3
  18.7 71.8 %all-reduce.7.cloned.1.call-done = (f32[64,512]{1,0:T(8,128)}, f32[64,512]{1,0:T(8,128)}) async-done(((f32[64,512]{1,0:T(8,128)}, f32[64,512]{1,0:T(8,128)}), (f32[64,512]{1,0:T(8,128)}, f32[64,512]{1,0:T(8,128)})) %all-reduce.7.cloned.1.call-update) | async-done | bytes 262160 | tf_op jit(solution)/shard_map/psum | solution.py:111
  90.5 0.8 slice_bitcast_fusion.3
  91.2 5.3 scatter_fusion
  96.6 5.3 scatter_fusion.1
  101.9 1.3 slice_bitcast_fusion.1
  103.6 133.3 %while.42 = (s32[]{:T(128)}, f32[64,2112]{1,0:T(8,128)S(1)}, s32[]{:T(128)}, f32[1,1]{1,0:T(1,128)}, s32[]{:T(128)}, /*index=5*/s32[]{:T(128)}, s32[]{:T(128)}) while((s32[]{:T(128)}, f32[64,2112]{1,0:T(8,128)S(1)}, s32[]{:T(128)}, f32[1,1]{1,0:T(1,128)}, s32[]{:T(128)}, /*index=5*/s32[]{:T(128)}, s32[]{:T(128)}) %tuple.128), condition=%wide.region_5.6_spmd.clone.clone, body=%wide.region_4.5_spmd.clone.clone.sunk | while | flops 547205 | bytes 2196437 | solution.py:33
  103.6 0.7 dynamic_slice.81
  105.7 0.7 dynamic_slice.81
  107.8 0.7 dynamic_slice.81
  109.9 0.7 dynamic_slice.81
  112.0 0.7 dynamic_slice.81
  114.0 0.7 dynamic_slice.81
  116.1 0.7 dynamic_slice.81
  118.2 0.7 dynamic_slice.81
  120.3 0.7 dynamic_slice.81
  122.4 0.7 dynamic_slice.81
  124.5 0.7 dynamic_slice.81
  126.5 0.7 dynamic_slice.81
  128.6 0.7 dynamic_slice.81
  130.7 0.7 dynamic_slice.81
  132.8 0.7 dynamic_slice.81
  134.9 0.7 dynamic_slice.81
  137.0 0.7 dynamic_slice.81
  139.0 0.7 dynamic_slice.81
  141.1 0.7 dynamic_slice.81
  143.2 0.7 dynamic_slice.81
  236.9 1.0 slice_select_fusion.1
  238.0 0.7 compare_reduce_fusion
  238.8 31.9 %all-gather.1 = f32[2048,64]{1,0:T(8,128)S(1)} all-gather(f32[64,64]{1,0:T(8,128)S(1)} %slice_select_fusion.7), channel_id=3, replica_groups=mesh['row'=8,'col'=32] {'col'}, dimensions={0}, use_global_device_ids=true | all-gather | bytes 540672 | tf_op jit(solution)/shard_map/all_gather | solution.py:12
  271.0 4.9 custom-call.4
  276.3 44.1 %all-gather.7.cloned.1.call-done = f32[2048,2048]{1,0:T(8,128)} async-done(((f32[64,2048]{1,0:T(8,128)}), f32[2048,2048]{1,0:T(8,128)}) %all-gather.7.cloned.1.call-update) | async-done | bytes 16777232 | tf_op jit(solution)/shard_map/all_gather | solution.py:12
  320.4 6.9 %reduce_sum.36 = f32[64,2048]{1,0:T(8,128)S(1)} reduce(f32[32,64,2048]{2,1,0:T(8,128)} %bitcast.138, f32[]{:T(128)} %constant.578.clone.1), dimensions={0}, to_apply=%region_6.7 | reduce | flops 4063232 | bytes 17301508 | tf_op jit(solution)/shard_map/reduce_sum | solution.py:12
  327.6 5.7 subtract_select_fusion.3
  333.3 2.0 copy-done
  335.3 1.0 select_select_fusion.1
  336.3 5.8 scatter.60
  342.1 1.6 constant_dynamic-update-slice_fusion.1
  343.7 2.8 scatter.62
  346.5 2.9 gather_fusion.3
  349.4 2.9 gather_fusion.2
  352.3 0.7 broadcast_select_fusion
  353.1 0.7 broadcast_select_fusion.1
  353.9 67.2 %all-reduce.5.cloned.1.call-done = (f32[64,512]{1,0:T(8,128)}, f32[64,512]{1,0:T(8,128)}) async-done(((f32[64,512]{1,0:T(8,128)}, f32[64,512]{1,0:T(8,128)}), (f32[64,512]{1,0:T(8,128)}, f32[64,512]{1,0:T(8,128)})) %all-reduce.5.cloned.1.call-update) | async-done | bytes 262160 | tf_op jit(solution)/shard_map/psum | solution.py:111
  421.0 0.8 slice_bitcast_fusion.2
  421.8 5.3 scatter_fusion.2
  427.1 5.3 scatter_fusion.3
  432.5 1.3 slice_bitcast_fusion
  434.2 133.3 %while.43 = (s32[]{:T(128)}, f32[64,2112]{1,0:T(8,128)S(1)}, s32[]{:T(128)}, f32[1,1]{1,0:T(1,128)}, s32[]{:T(128)}, /*index=5*/s32[]{:T(128)}, s32[]{:T(128)}) while((s32[]{:T(128)}, f32[64,2112]{1,0:T(8,128)S(1)}, s32[]{:T(128)}, f32[1,1]{1,0:T(1,128)}, s32[]{:T(128)}, /*index=5*/s32[]{:T(128)}, s32[]{:T(128)}) %tuple.131), condition=%wide.region_14.16_spmd.clone.clone, body=%wide.region_13.15_spmd.clone.clone.sunk | while | flops 547205 | bytes 2196437 | solution.py:33
  567.5 1.0 slice_select_fusion
  568.6 32.2 %all-gather.3 = f32[2048,64]{1,0:T(8,128)S(1)} all-gather(f32[64,64]{1,0:T(8,128)S(1)} %slice_select_fusion.6), channel_id=5, replica_groups=mesh['row'=8,'col'=32] {'col'}, dimensions={0}, use_global_device_ids=true | all-gather | bytes 540672 | tf_op jit(solution)/shard_map/all_gather | solution.py:12
  601.1 4.9 custom-call.5
  606.3 44.8 %all-gather.9.cloned.1.call-done = f32[2048,2048]{1,0:T(8,128)} async-done(((f32[64,2048]{1,0:T(8,128)}), f32[2048,2048]{1,0:T(8,128)}) %all-gather.9.cloned.1.call-update) | async-done | bytes 16777232 | tf_op jit(solution)/shard_map/all_gather | solution.py:12
  651.1 6.9 %reduce_sum.38 = f32[64,2048]{1,0:T(8,128)S(1)} reduce(f32[32,64,2048]{2,1,0:T(8,128)} %bitcast.139, f32[]{:T(128)} %constant.578.clone.1), dimensions={0}, to_apply=%region_15.17 | reduce | flops 4063232 | bytes 17301508 | tf_op jit(solution)/shard_map/reduce_sum | solution.py:12
  658.4 5.7 subtract_select_fusion.2
  664.1 2.0 copy-done.1
  666.1 1.0 select_select_fusion
  667.1 5.8 scatter.65
  672.9 1.6 constant_dynamic-update-slice_fusion
  674.5 2.8 scatter.67
  (929 shorter events, 155.4 us)
Async XLA Ops:
  6.5 4.7 copy-start.4
  6.5 83.9 %all-reduce.7.cloned.1.call-start = ((), (), s32[]{:S(2)}) async-start(), calls=%async_computation.3 | async-start | bytes 524288 | tf_op jit(solution)/shard_map/psum | solution.py:111
  18.6 301.8 %all-gather.7.cloned.1.call-start = ((), (), s32[]{:S(2)}) async-start(), calls=%async_computation | async-start | bytes 17301504 | tf_op jit(solution)/shard_map/all_gather | solution.py:12
  103.6 172.3 %copy-start.2 = (f32[64,512]{1,0:T(8,128)S(1)}, f32[64,512]{1,0:T(8,128)}, u32[]{:S(2)}) copy-start(f32[64,512]{1,0:T(8,128)} %get-tuple-element.390) | copy-start | bytes 393220
  238.0 183.1 %all-reduce.5.cloned.1.call-start = ((), (), s32[]{:S(2)}) async-start(), calls=%async_computation.2 | async-start | bytes 524288 | tf_op jit(solution)/shard_map/psum | solution.py:111
  333.3 2.0 copy-start
  353.8 297.3 %all-gather.9.cloned.1.call-start = ((), (), s32[]{:S(2)}) async-start(), calls=%async_computation.1 | async-start | bytes 17301504 | tf_op jit(solution)/shard_map/all_gather | solution.py:12
  434.2 171.8 %copy-start.3 = (f32[64,512]{1,0:T(8,128)S(1)}, f32[64,512]{1,0:T(8,128)}, u32[]{:S(2)}) copy-start(f32[64,512]{1,0:T(8,128)} %get-tuple-element.388) | copy-start | bytes 393220
  664.1 2.0 copy-start.1
Sparse Core Ops, SparseCore 0:
  18.7 71.6 all-reduce.6
  238.1 82.2 all-gather.6
  353.9 67.0 all-reduce.4
  568.7 82.4 all-gather.8
